TPU v7x, 512 devices: a whole 4x4x16 slice. The times are simulated.
512 devices in a mesh: domain: 64 (over x, y, z_lo), member: 8 (over z_hi, core).
Axes of the slice: x: 4, y: 4, z: 16 (z_hi: 4, z_lo: 4; z = z_hi * 4 + z_lo), core: 2. Of those that a mesh axis runs over, the one named last changes fastest.
Arguments:
- inputs: bfloat16 [16, 12288, 1024], P('member', 'domain')
- norm_gain: bfloat16 [1024], P('member'), may hold values from 0.099609375 to 1.8984375
- w_query: bfloat16 [1024, 512], P('member')
- w_key: bfloat16 [1024, 512], P('member')
- w_value: bfloat16 [1024, 512], P('member'), may hold values from -0.1875 to 0.1875
- w_out: bfloat16 [512, 1024], P('member'), may hold values from -0.75 to 0.75
- neighbors: int32 [192, 9], P('domain'), may hold values from 0 to 191, as said below
- slot_valid: int32 [192, 9], P('domain'), may hold values from 0 to 1, as said below
- output_cotangent: bfloat16 [16, 12288, 1024], P('member', 'domain'), may hold values from -1.5 to 1.5
Outputs:
- attn_out: bfloat16 [16, 12288, 1024], P('member', 'domain')
- d_input: bfloat16 [16, 12288, 1024], P('member', 'domain')
- grad_wout: float32 [512, 1024], P('member')
Inputs may be any that keep to these rules, and one draw needn't show every extreme that they name: `neighbors`: slot 0 of block b names b. The blocks named by the valid slots of b are distinct and lie within blocks (b // 3 - 1) * 3 to (b // 3 + 2) * 3 - 1. An invalid slot names b. `slot_valid`: slot 0 is always 1.
All inputs are finite; a program needn't handle non-finite values.
Results may differ from a plain program's by a relative error of at most 0.019.
Values may be sent and summed in bfloat16 or wider, within the bound.
No kernel may reach another device: no remote copies, remote signals or barrier semaphores. Data moves between devices by JAX's collectives and lax.ppermute only.
A program may use at most 128 MiB of HBM per device.

v0:
```python
import jax
import jax.numpy as jnp
from jax import lax
from jax.sharding import PartitionSpec as P

HEAD_DIM = 64
EPSILON = 1e-06
MASKED = -1e30


def extended_2(value, sides, width):
    for axis, dim in sides:
        peers, length = (lax.axis_size(axis), value.shape[dim])
        up = [(i, (i + 1) % peers) for i in range(peers - 1)]
        down = [(j, i) for i, j in up]
        last = lax.slice_in_dim(value, length - width, length, axis=dim)
        initial = lax.slice_in_dim(value, 0, width, axis=dim)
        before = lax.ppermute(last, axis, up)
        after = lax.ppermute(initial, axis, down)
        value = jnp.concatenate([before, value, after], axis=dim)
    return value


def pair_columns(field, pair_index, pair_width):
    return lax.dynamic_slice_in_dim(field, pair_index * pair_width, pair_width, field.ndim - 1)


def shards(
    inputs, norm_gain, w_query, w_key, w_value, w_out, neighbors, slot_valid, output_cotangent
):
    samples, length, model_width = inputs.shape
    block_count, slot_count = neighbors.shape
    block_len = length // block_count
    window_blocks = 3 * block_count
    full_gain, complete_query, complete_key, complete_value, complete_output = (
        lax.all_gather(norm_gain, "member", axis=0, tiled=True),
        lax.all_gather(w_query, "member", axis=0, tiled=True),
        lax.all_gather(w_key, "member", axis=0, tiled=True),
        lax.all_gather(w_value, "member", axis=0, tiled=True),
        lax.all_gather(w_out, "member", axis=0, tiled=True),
    )
    hidden_width = complete_query.shape[1]
    pair_width = 2 * HEAD_DIM
    pair_count = hidden_width // pair_width
    score_scale = HEAD_DIM ** (-0.5)
    inputs_float = inputs.astype(jnp.float32)
    inverse_rms = lax.rsqrt(jnp.mean(inputs_float * inputs_float, axis=-1, keepdims=True) + EPSILON)
    gain_float = full_gain.astype(jnp.float32)
    normalized_input = (inputs_float * inverse_rms * gain_float).astype(jnp.bfloat16)
    query = jnp.einsum(
        "fbi,iy->fby", normalized_input, complete_query, preferred_element_type=jnp.float32
    ).astype(jnp.bfloat16)
    key_rows = jnp.einsum(
        "fbi,iy->fby", normalized_input, complete_key, preferred_element_type=jnp.float32
    ).astype(jnp.bfloat16)
    value_rows = jnp.einsum(
        "fbi,iy->fby", normalized_input, complete_value, preferred_element_type=jnp.float32
    ).astype(jnp.bfloat16)
    key_value = jnp.concatenate([key_rows, value_rows], axis=-1)
    extended = extended_2(key_value, (("domain", 1),), length)
    domain_rank = lax.axis_index("domain")
    local_index = neighbors - (domain_rank - 1) * block_count
    present = slot_valid > 0
    window_ids = jnp.arange(window_blocks, dtype=jnp.int32)
    key_all = extended[..., :hidden_width]
    value_all = extended[..., hidden_width:]
    score_spec = "sbqgd,skgd->sbgqk"
    mix_spec = "sbgqk,skgd->sbqgd"
    back_spec = "sbgqk,sbqgd->skgd"
    matches = jnp.logical_and(
        local_index[:, :, None] == window_ids[None, None, :], present[:, :, None]
    )
    included = jnp.any(matches, axis=1)
    key_mask = jnp.repeat(included, block_len, axis=1)

    def pair_keys(pair_index):
        key_pair = pair_columns(key_all, pair_index, pair_width).reshape(
            samples, window_blocks * block_len, 2, HEAD_DIM
        )
        value_pair = pair_columns(value_all, pair_index, pair_width).reshape(
            samples, window_blocks * block_len, 2, HEAD_DIM
        )
        return (key_pair, value_pair)

    def to_window(grad_keys):
        return grad_keys.reshape(samples, window_blocks * block_len, pair_width)

    def pair_probability(pair_index):
        query_pair = pair_columns(query, pair_index, pair_width).reshape(
            samples, block_count, block_len, 2, HEAD_DIM
        )
        key_pair, value_pair = pair_keys(pair_index)
        scores = (
            jnp.einsum(score_spec, query_pair, key_pair, preferred_element_type=jnp.float32)
            * score_scale
        )
        scores = jnp.where(key_mask[None, :, None, None, :], scores, MASKED)
        row_max = jnp.max(scores, axis=-1, keepdims=True)
        shifted = jnp.exp(scores - row_max)
        probability = shifted / jnp.sum(shifted, axis=-1, keepdims=True)
        return (query_pair, key_pair, value_pair, probability)

    def forward_pair(pair_index):
        query_pair, key_pair, value_pair, probability = pair_probability(pair_index)
        prob_bf = probability.astype(jnp.bfloat16)
        mixed_pair = jnp.einsum(mix_spec, prob_bf, value_pair, preferred_element_type=jnp.float32)
        return mixed_pair.astype(jnp.bfloat16).reshape(samples, length, pair_width)

    attention_pairs = lax.map(forward_pair, jnp.arange(pair_count))
    neighbour_attention = jnp.transpose(attention_pairs, (1, 2, 0, 3)).reshape(
        samples, length, hidden_width
    )
    attn_out = jnp.einsum(
        "qny,yb->qnb", neighbour_attention, complete_output, preferred_element_type=jnp.float32
    ).astype(jnp.bfloat16)
    d_attention = jnp.einsum(
        "yjz,bz->yjb", output_cotangent, complete_output, preferred_element_type=jnp.float32
    ).astype(jnp.bfloat16)
    row_share = hidden_width // lax.axis_size("member")
    member_total = samples * lax.axis_size("member")
    incomplete_gradient = jnp.einsum(
        "rfe,rfu->eu", neighbour_attention, output_cotangent, preferred_element_type=jnp.float32
    )
    total_grad = lax.psum(incomplete_gradient, ("domain", "member"))
    grad_mine = lax.dynamic_slice_in_dim(
        total_grad, lax.axis_index("member") * row_share, row_share, 0
    )
    grad_wout = grad_mine / member_total

    def backward_pair(pair_index):
        query_pair, key_pair, value_pair, probability = pair_probability(pair_index)
        prob_bf = probability.astype(jnp.bfloat16)
        grad_pair = pair_columns(d_attention, pair_index, pair_width).reshape(
            samples, block_count, block_len, 2, HEAD_DIM
        )
        d_prob = jnp.einsum(score_spec, grad_pair, value_pair, preferred_element_type=jnp.float32)
        delta = jnp.sum(probability * d_prob, axis=-1, keepdims=True)
        d_score = (probability * (d_prob - delta) * score_scale).astype(jnp.bfloat16)
        d_query_pair = jnp.einsum(mix_spec, d_score, key_pair, preferred_element_type=jnp.float32)
        d_query_pair = d_query_pair.astype(jnp.bfloat16).reshape(samples, length, pair_width)
        d_key_pair = jnp.einsum(back_spec, d_score, query_pair, preferred_element_type=jnp.float32)
        d_value_pair = jnp.einsum(back_spec, prob_bf, grad_pair, preferred_element_type=jnp.float32)
        return (d_query_pair, to_window(d_key_pair), to_window(d_value_pair))

    query_grads, key_grads, value_grads = lax.map(backward_pair, jnp.arange(pair_count))
    query_cotangent = jnp.transpose(query_grads, (1, 2, 0, 3)).reshape(
        samples, length, hidden_width
    )
    key_ext = jnp.transpose(key_grads, (1, 2, 0, 3)).reshape(samples, 3 * length, hidden_width)
    value_ext = jnp.transpose(value_grads, (1, 2, 0, 3)).reshape(samples, 3 * length, hidden_width)
    ext_grad = jnp.concatenate([key_ext, value_ext], axis=-1)
    lower_rim = ext_grad[:, :length]
    own_part = ext_grad[:, length : 2 * length]
    upper_rim = ext_grad[:, 2 * length :]
    rims_half = jnp.concatenate([lower_rim, upper_rim], axis=1).astype(jnp.bfloat16)
    returned = extended_2(rims_half, (("domain", 1),), length)
    from_below = returned[:, :length].astype(jnp.float32)
    from_above = returned[:, 3 * length :].astype(jnp.float32)
    kv_total = own_part + from_below + from_above
    kv_grad = kv_total.astype(jnp.bfloat16)
    key_cotangent = kv_grad[..., :hidden_width]
    value_cotangent = kv_grad[..., hidden_width:]
    normed_cotangent = jnp.einsum(
        "qja,ga->qjg", query_cotangent, complete_query, preferred_element_type=jnp.float32
    )
    normed_cotangent = normed_cotangent + jnp.einsum(
        "qja,ga->qjg", key_cotangent, complete_key, preferred_element_type=jnp.float32
    )
    normed_cotangent = normed_cotangent + jnp.einsum(
        "qja,ga->qjg", value_cotangent, complete_value, preferred_element_type=jnp.float32
    )
    scaled_grad = normed_cotangent * gain_float
    inner_mean = jnp.mean(scaled_grad * inputs_float, axis=-1, keepdims=True)
    d_input = inverse_rms * scaled_grad - inputs_float * inverse_rms**3 * inner_mean
    return (attn_out, d_input.astype(jnp.bfloat16), grad_wout)


def solution(mesh):
    placed = (
        P("member", "domain", None),
        P("member"),
        P("member", None),
        P("member", None),
        P("member", None),
        P("member", None),
        P("domain", None),
        P("domain", None),
        P("member", "domain", None),
    )
    return jax.shard_map(
        shards,
        mesh=mesh,
        in_specs=placed,
        out_specs=(P("member", "domain", None), P("member", "domain", None), P("member", None)),
        check_vma=False,
    )
```

profile of v0, /device:TPU:1, one launch (start us, length us, event | category | flops | bytes accessed | tf_op | source)
XLA Modules:
  0.0 901.7 jit_solution(3319372591805515954)
XLA Ops:
  11.5 22.8 %all-gather = bf16[8,1,128]{2,1,0:T(2,128)(2,1)S(1)} all-gather(bf16[1,1,128]{2,1,0:T(2,128)(2,1)} %bitcast.205), channel_id=1, replica_groups=mesh['domain'=64,'member'=8] {'member'}, dimensions={0}, use_global_device_ids=true | all-gather | bytes 2304 | tf_op jit(solution)/shard_map/all_gather | solution.py:36
  35.0 28.1 %all-gather.8.cloned.1.call-done = bf16[1024,512]{1,0:T(8,128)(2,1)} async-done(((bf16[128,512]{1,0:T(8,128)(2,1)}), bf16[1024,512]{1,0:T(8,128)(2,1)}) %all-gather.8.cloned.1.call-update) | async-done | bytes 1048592 | tf_op jit(solution)/shard_map/all_gather | solution.py:39
  63.1 2.1 convolution_convert_fusion.4
  65.2 42.2 %all-gather.6.cloned.1.call-done = bf16[1024,512]{1,0:T(8,128)(2,1)} async-done(((bf16[128,512]{1,0:T(8,128)(2,1)}), bf16[1024,512]{1,0:T(8,128)(2,1)}) %all-gather.6.cloned.1.call-update) | async-done | bytes 1048592 | tf_op jit(solution)/shard_map/all_gather | solution.py:38
  107.3 1.8 convolution_convert_fusion.5
  111.5 4.9 collective-permute-start
  116.7 37.4 %all-gather.12.cloned.1.call-done = bf16[512,1024]{1,0:T(8,128)(2,1)} async-done(((bf16[64,1024]{1,0:T(8,128)(2,1)}), bf16[512,1024]{1,0:T(8,128)(2,1)}) %all-gather.12.cloned.1.call-update) | async-done | bytes 1048592 | tf_op jit(solution)/shard_map/all_gather | solution.py:40
  154.0 2.6 convolution_convert_fusion.2
  156.6 59.6 %all-gather.10.cloned.1.call-done = bf16[1024,512]{1,0:T(8,128)(2,1)} async-done(((bf16[128,512]{1,0:T(8,128)(2,1)}), bf16[1024,512]{1,0:T(8,128)(2,1)}) %all-gather.10.cloned.1.call-update) | async-done | bytes 1048592 | tf_op jit(solution)/shard_map/all_gather | solution.py:37
  216.2 2.6 convolution_convert_fusion.3
  224.2 34.7 %while.26 = (s32[]{:T(128)}, bf16[4,2,192,128]{3,2,1,0:T(8,128)(2,1)}, s32[4]{0:T(128)S(1)}, bf16[2,576,512]{1,2,0:T(8,128)(2,1)}, bf16[2,576,512]{1,2,0:T(8,128...) while((s32[]{:T(128)}, ...), condition=%wide.region_5.6_spmd.clone, body=%wide.region_2.5_spmd.clone.sunk | while | flops 117278592 | bytes 8469142 | solution.py:109
  228.9 2.2 fusion.129
  237.5 2.2 fusion.129
  246.2 2.2 fusion.129
  254.9 2.2 fusion.129
  259.7 121.8 %while.27 = (s32[]{:T(128)}, bf16[4,2,192,128]{3,2,1,0:T(8,128)(2,1)}, f32[4,2,576,128]{2,3,1,0:T(8,128)}, f32[4,2,576,128]{2,3,1,0:T(8,128)}, s32[4]{0:T(128)S(...) while((s32[]{:T(128)}, ...), condition=%wide.region_10.11_spmd.clone, body=%wide.region_6.0_spmd.clone.sunk | while | flops 293343744 | bytes 26301140 | solution.py:145
  264.0 1.7 fusion.140
  267.3 1.8 fusion.142
  269.1 7.8 fusion.143
  278.8 2.4 fusion.144
  281.2 7.7 fusion.145
  294.4 1.7 fusion.140
  297.8 1.8 fusion.142
  299.5 7.8 fusion.143
  309.2 2.4 fusion.144
  311.6 7.7 fusion.145
  328.1 1.8 fusion.142
  329.9 7.8 fusion.143
  339.6 2.4 fusion.144
  342.0 7.7 fusion.145
  355.3 1.7 fusion.140
  358.6 1.8 fusion.142
  360.4 7.8 fusion.143
  370.1 2.4 fusion.144
  372.5 7.7 fusion.145
  381.4 3.2 copy.65
  384.7 2.1 reshape.81
  386.8 3.5 constant_dynamic-update-slice_fusion.5
  390.2 2.6 copy.66
  392.8 2.7 reshape.82
  395.5 1.7 constant_dynamic-update-slice_fusion.4
  397.3 2.7 convert.6
  402.3 4.9 collective-permute-start.2
  407.2 2.1 convolution_bitcast_fusion
  409.3 2.8 convolution_convert_fusion.1
  412.7 9.3 %collective-permute-done.3 = bf16[2,192,1024]{2,1,0:T(8,128)(2,1)} collective-permute-done((bf16[2,192,1024]{2,1,0:T(8,128)(2,1)}, bf16[2,192,1024]{2,1,0:T(8,128)(2,1)}, u32[]{:S(2)}, u32[]{:S(2)}) %collective-permute-start.3) | collective-permute-done | bytes 786464 | tf_op jit(solution)/shard_map/ppermute | solution.py:19
  422.6 2.2 fusion.58
  428.5 465.0 %all-reduce.2.cloned.1.call-done = f32[512,1024]{1,0:T(8,128)} async-done(((f32[512,1024]{1,0:T(8,128)}), f32[512,1024]{1,0:T(8,128)}) %all-reduce.2.cloned.1.call-update) | async-done | bytes 2097168 | tf_op jit(solution)/shard_map/psum | solution.py:124
  (182 shorter events, 80.6 us)
Async XLA Ops:
  7.2 146.9 %copy-start = (bf16[2,192,1024]{2,1,0:T(8,128)(2,1)S(1)}, bf16[2,192,1024]{2,1,0:T(8,128)(2,1)}, u32[]{:S(2)}) copy-start(bf16[2,192,1024]{2,1,0:T(8,128)(2,1)} %param.21) | copy-start | bytes 2359300
  7.2 55.9 %all-gather.8.cloned.1.call-start = ((), (), s32[]{:S(2)}) async-start(), calls=%async_computation.1 | async-start | bytes 1179648 | tf_op jit(solution)/shard_map/all_gather | solution.py:39
  7.9 99.4 %all-gather.6.cloned.1.call-start = ((), (), s32[]{:S(2)}) async-start(), calls=%async_computation | async-start | bytes 1179648 | tf_op jit(solution)/shard_map/all_gather | solution.py:38
  8.7 145.4 %all-gather.12.cloned.1.call-start = ((), (), s32[]{:S(2)}) async-start(), calls=%async_computation.3 | async-start | bytes 1179648 | tf_op jit(solution)/shard_map/all_gather | solution.py:40
  9.4 206.8 %all-gather.10.cloned.1.call-start = ((), (), s32[]{:S(2)}) async-start(), calls=%async_computation.2 | async-start | bytes 1179648 | tf_op jit(solution)/shard_map/all_gather | solution.py:37
  10.0 97.4 %copy-start.2 = (bf16[2,192,1024]{2,1,0:T(8,128)(2,1)S(1)}, bf16[2,192,1024]{2,1,0:T(8,128)(2,1)}, u32[]{:S(2)}) copy-start(bf16[2,192,1024]{2,1,0:T(8,128)(2,1)} %param.13) | copy-start | bytes 2359300
  10.0 883.5 %all-reduce.2.cloned.1.call-start = ((), (), s32[]{:S(2)}) async-start(), calls=%async_computation.4 | async-start | bytes 4194304 | tf_op jit(solution)/shard_map/psum | solution.py:124
  65.1 51.2 %copy-start.10 = (s32[3,9]{1,0:T(4,128)S(1)}, s32[3,9]{1,0:T(4,128)}, u32[]{:S(2)}) copy-start(s32[3,9]{1,0:T(4,128)} %param.20) | copy-start | bytes 328
  110.2 108.6 %collective-permute-start.1 = (bf16[2,192,1024]{2,1,0:T(8,128)(2,1)}, bf16[2,192,1024]{2,1,0:T(8,128)(2,1)S(1)}, u32[]{:S(2)}, u32[]{:S(2)}) collective-permute-start(bf16[2,192,1024]{2,1,0:T(8,128)(2,1)} %pad_maximum_fusion.1), channel_id=1, source_target_pairs={{8,0},{16,8},{24,16},{32,24},{40,32},{48,40},{56,48},{64,56},{72,6... | collective-permute-start | bytes 2359304 | tf_op jit(solution)/shard_map/ppermute | solution.py:19
  111.5 107.3 %collective-permute-start = (bf16[2,192,1024]{2,1,0:T(8,128)(2,1)}, bf16[2,192,1024]{2,1,0:T(8,128)(2,1)}, u32[]{:S(2)}, u32[]{:S(2)}) collective-permute-start(bf16[2,192,1024]{2,1,0:T(8,128)(2,1)} %pad_maximum_fusion.1), channel_id=1, source_target_pairs={{0,8},{8,16},{16,24},{24,32},{32,40},{40,48},{48,56},{56,64},{64,7... | collective-permute-start | bytes 2359304 | tf_op jit(solution)/shard_map/ppermute | solution.py:18
  281.2 7.7 copy-start.1
  311.6 7.7 copy-start.1
  342.0 7.7 copy-start.1
  372.5 7.7 copy-start.1
  386.8 3.5 copy-start.4
  400.0 7.2 copy-start.5
  401.0 21.0 %collective-permute-start.3 = (bf16[2,192,1024]{2,1,0:T(8,128)(2,1)}, bf16[2,192,1024]{2,1,0:T(8,128)(2,1)}, u32[]{:S(2)}, u32[]{:S(2)}) collective-permute-start(bf16[2,192,1024]{2,1,0:T(8,128)(2,1)} %get-tuple-element.247), channel_id=1, source_target_pairs={{8,0},{16,8},{24,16},{32,24},{40,32},{48,40},{56,48},{64,56},{72,6... | collective-permute-start | bytes 2359304 | tf_op jit(solution)/shard_map/ppermute | solution.py:19
  402.3 20.3 %collective-permute-start.2 = (bf16[2,192,1024]{2,1,0:T(8,128)(2,1)S(1)}, bf16[2,192,1024]{2,1,0:T(8,128)(2,1)}, u32[]{:S(2)}, u32[]{:S(2)}) collective-permute-start(bf16[2,192,1024]{2,1,0:T(8,128)(2,1)S(1)} %get-tuple-element.246), channel_id=1, source_target_pairs={{0,8},{8,16},{16,24},{24,32},{32,40},{40,48},{48,56},{56,64},{64,7... | collective-permute-start | bytes 2359304 | tf_op jit(solution)/shard_map/ppermute | solution.py:18
  409.3 2.8 copy-start.6
  409.3 2.8 copy-start.8
  412.7 12.2 %copy-start.7 = (bf16[1024,512]{1,0:T(8,128)(2,1)S(1)}, bf16[1024,512]{1,0:T(8,128)(2,1)}, u32[]{:S(2)}) copy-start(bf16[1024,512]{1,0:T(8,128)(2,1)} %all-gather.6.cloned.1.call-done) | copy-start | bytes 3145732
  424.9 1.1 copy-start.3
  424.9 1.5 copy-start.9
Sparse Core Ops, SparseCore 0:
  10.1 52.8 all-gather.7
  65.2 42.0 all-gather.5
  109.5 44.4 all-gather.11
  156.0 60.1 all-gather.9
  409.4 484.0 all-reduce.1
where the time goes:
time: 903 us; the launch traced here: 902 us
  waiting for transfers between devices  645 us (71%)
  matrix products  106 us (12%)
  local copies, waits for them, and re-layouts  73.6 us (8%)
  blocking collectives  22.8 us (3%)
  other arithmetic  22.2 us (2%)
  between operations  14 us (2%)
  starting transfers between devices  12.5 us (1%)
    psum x1, waiting for transfers between devices, shards(): total_grad = lax.psum(incomplete_gradient, ('domain', 'member'))  465 us
    all_gather x1, waiting for transfers between devices, shards(): lax.all_gather(w_query, 'member', axis=0, tiled=True)  59.6 us
    all_gather x1, waiting for transfers between devices, shards(): lax.all_gather(w_key, 'member', axis=0, tiled=True)  42.2 us
    all_gather x1, waiting for transfers between devices, shards(): lax.all_gather(w_out, 'member', axis=0, tiled=True)  37.4 us
    dot_general x4, matrix products, backward_pair(): jnp.einsum(mix_spec, d_score, key_pair, preferred_element_type=jnp.float32)  31.3 us
    dot_general x4, matrix products, backward_pair(): jnp.einsum(back_spec, d_score, query_pair, preferred_element_type=jnp.flo...  30.7 us
    all_gather x1, waiting for transfers between devices, shards(): lax.all_gather(w_value, 'member', axis=0, tiled=True)  28.1 us
    dynamic_slice x24, local copies, waits for them, and re-layouts, pair_columns(): lax.dynamic_slice_in_dim(field, pair_index * pair_width, pair_width, fiel...  23.5 us
  transfers between devices with their start and end apart: 9, of which 7 were waited for; matrix products, arithmetic and copies ran while one was open for 3% of the time, Pallas kernels for 0%

commit v1 on v0

--- a/solution.py
+++ b/solution.py
@@ -121,7 +121,7 @@
     incomplete_gradient = jnp.einsum(
         "rfe,rfu->eu", neighbour_attention, output_cotangent, preferred_element_type=jnp.float32
     )
-    total_grad = lax.psum(incomplete_gradient, ("domain", "member"))
+    total_grad = lax.psum(lax.psum(incomplete_gradient, "domain"), "member")
     grad_mine = lax.dynamic_slice_in_dim(
         total_grad, lax.axis_index("member") * row_share, row_share, 0
     )

time: 903 us -> 1140 us (1.26)
  waiting for transfers between devices: 645 us -> 890 us
    psum x1 -> x2, waiting for transfers between devices: 465 us -> 721 us  [shards(): total_grad = lax.psum(lax.psum(incomplete_gradient, 'domain'), 'member')]
  transfers between devices with their start and end apart: 9 -> 10, of which waited for: 7 -> 6; matrix products, arithmetic and copies ran while one was open for 3% -> 13% of each run, Pallas kernels for 0% -> 0%
where the time goes in v1:
time: 1140 us
  waiting for transfers between devices  890 us (78%)
  matrix products  106 us (9%)
  local copies, waits for them, and re-layouts  68.9 us (6%)
  blocking collectives  22.8 us (2%)
  other arithmetic  20.4 us (2%)
  between operations  14.3 us (1%)
  starting transfers between devices  12.8 us (1%)
    psum x2, waiting for transfers between devices, shards(): total_grad = lax.psum(lax.psum(incomplete_gradient, 'domain'), 'member')  721 us
    all_gather x1, waiting for transfers between devices, shards(): lax.all_gather(w_query, 'member', axis=0, tiled=True)  59.6 us
    all_gather x1, waiting for transfers between devices, shards(): lax.all_gather(w_key, 'member', axis=0, tiled=True)  42.2 us
    all_gather x1, waiting for transfers between devices, shards(): lax.all_gather(w_out, 'member', axis=0, tiled=True)  37.3 us
    dot_general x4, matrix products, backward_pair(): jnp.einsum(back_spec, d_score, query_pair, preferred_element_type=jnp.flo...  31.2 us
    dot_general x4, matrix products, backward_pair(): jnp.einsum(mix_spec, d_score, key_pair, preferred_element_type=jnp.float32)  29.6 us
    all_gather x1, waiting for transfers between devices, shards(): lax.all_gather(w_value, 'member', axis=0, tiled=True)  28.1 us
    dynamic_slice x24, local copies, waits for them, and re-layouts, pair_columns(): lax.dynamic_slice_in_dim(field, pair_index * pair_width, pair_width, fiel...  23.5 us
  transfers between devices with their start and end apart: 10, of which 6 were waited for; matrix products, arithmetic and copies ran while one was open for 13% of the time, Pallas kernels for 0%

profile of v1, /device:TPU:1, one launch (start us, length us, event | category | flops | bytes accessed | tf_op | source)
XLA Modules:
  0.0 1141.4 jit_solution(14979146941698480643)
XLA Ops:
  11.5 22.8 %all-gather = bf16[8,1,128]{2,1,0:T(2,128)(2,1)S(1)} all-gather(bf16[1,1,128]{2,1,0:T(2,128)(2,1)} %bitcast.205), channel_id=1, replica_groups=mesh['domain'=64,'member'=8] {'member'}, dimensions={0}, use_global_device_ids=true | all-gather | bytes 2304 | tf_op jit(solution)/shard_map/all_gather | solution.py:36
  35.0 28.1 %all-gather.8.cloned.1.call-done = bf16[1024,512]{1,0:T(8,128)(2,1)} async-done(((bf16[128,512]{1,0:T(8,128)(2,1)}), bf16[1024,512]{1,0:T(8,128)(2,1)}) %all-gather.8.cloned.1.call-update) | async-done | bytes 1048592 | tf_op jit(solution)/shard_map/all_gather | solution.py:39
  63.1 2.1 convolution_convert_fusion.4
  65.2 42.2 %all-gather.6.cloned.1.call-done = bf16[1024,512]{1,0:T(8,128)(2,1)} async-done(((bf16[128,512]{1,0:T(8,128)(2,1)}), bf16[1024,512]{1,0:T(8,128)(2,1)}) %all-gather.6.cloned.1.call-update) | async-done | bytes 1048592 | tf_op jit(solution)/shard_map/all_gather | solution.py:38
  107.3 1.8 convolution_convert_fusion.5
  111.5 4.9 collective-permute-start
  116.7 37.3 %all-gather.12.cloned.1.call-done = bf16[512,1024]{1,0:T(8,128)(2,1)} async-done(((bf16[64,1024]{1,0:T(8,128)(2,1)}), bf16[512,1024]{1,0:T(8,128)(2,1)}) %all-gather.12.cloned.1.call-update) | async-done | bytes 1048592 | tf_op jit(solution)/shard_map/all_gather | solution.py:40
  154.0 2.6 convolution_convert_fusion.2
  156.6 59.6 %all-gather.10.cloned.1.call-done = bf16[1024,512]{1,0:T(8,128)(2,1)} async-done(((bf16[128,512]{1,0:T(8,128)(2,1)}), bf16[1024,512]{1,0:T(8,128)(2,1)}) %all-gather.10.cloned.1.call-update) | async-done | bytes 1048592 | tf_op jit(solution)/shard_map/all_gather | solution.py:37
  216.2 2.6 convolution_convert_fusion.3
  224.1 34.7 %while.26 = (s32[]{:T(128)}, bf16[4,2,192,128]{3,2,1,0:T(8,128)(2,1)}, s32[4]{0:T(128)S(1)}, bf16[2,576,512]{1,2,0:T(8,128)(2,1)}, bf16[2,576,512]{1,2,0:T(8,128...) while((s32[]{:T(128)}, ...), condition=%wide.region_5.6_spmd.clone, body=%wide.region_2.5_spmd.clone.sunk | while | flops 117278592 | bytes 8469142 | solution.py:109
  228.8 2.2 fusion.129
  237.4 2.2 fusion.129
  246.1 2.2 fusion.129
  254.8 2.2 fusion.129
  258.8 3.0 convolution_bitcast_fusion
  262.1 115.1 %while.27 = (s32[]{:T(128)}, bf16[4,2,192,128]{3,2,1,0:T(8,128)(2,1)S(1)}, f32[4,2,576,128]{2,3,1,0:T(8,128)}, f32[4,2,576,128]{2,3,1,0:T(8,128)}, s32[4]{0:T(12...) while((s32[]{:T(128)}, ...), condition=%wide.region_10.11_spmd.clone, body=%wide.region_6.0_spmd.clone.sunk | while | flops 293343744 | bytes 26301140 | solution.py:145
  266.5 1.7 fusion.140
  269.9 1.9 fusion.142
  271.8 7.4 fusion.143
  279.5 2.4 fusion.144
  281.9 7.8 fusion.145
  295.3 1.7 fusion.140
  298.6 1.9 fusion.142
  300.6 7.4 fusion.143
  308.3 2.4 fusion.144
  310.7 7.8 fusion.145
  324.0 1.7 fusion.140
  327.4 1.9 fusion.142
  329.3 7.4 fusion.143
  337.0 2.4 fusion.144
  339.4 7.8 fusion.145
  352.8 1.7 fusion.140
  356.2 1.9 fusion.142
  358.1 7.4 fusion.143
  365.8 2.4 fusion.144
  368.2 7.8 fusion.145
  377.2 4.1 copy.65
  381.3 2.7 reshape.81
  384.0 4.1 copy.66
  388.1 3.6 reshape.82
  394.1 1.7 copy-done.3
  398.1 4.9 collective-permute-start.2
  403.0 546.2 %all-reduce.3.cloned.1.call-done = f32[512,1024]{1,0:T(8,128)} async-done(((f32[512,1024]{1,0:T(8,128)}), f32[512,1024]{1,0:T(8,128)}) %all-reduce.3.cloned.1.call-update) | async-done | bytes 2097168 | tf_op jit(solution)/shard_map/psum | solution.py:124
  949.3 2.8 convolution_convert_fusion.1
  952.7 2.3 fusion.58
  958.5 174.4 %all-reduce.5.cloned.1.call-done = f32[512,1024]{1,0:T(8,128)} async-done(((f32[512,1024]{1,0:T(8,128)}), f32[512,1024]{1,0:T(8,128)}) %all-reduce.5.cloned.1.call-update) | async-done | bytes 2097168 | tf_op jit(solution)/shard_map/psum | solution.py:124
  1132.9 1.7 dynamic-slice_multiply_fusion
  (187 shorter events, 72.1 us)
Async XLA Ops:
  7.2 146.9 %copy-start = (bf16[2,192,1024]{2,1,0:T(8,128)(2,1)S(1)}, bf16[2,192,1024]{2,1,0:T(8,128)(2,1)}, u32[]{:S(2)}) copy-start(bf16[2,192,1024]{2,1,0:T(8,128)(2,1)} %param.21) | copy-start | bytes 2359300
  7.2 55.9 %all-gather.8.cloned.1.call-start = ((), (), s32[]{:S(2)}) async-start(), calls=%async_computation.1 | async-start | bytes 1179648 | tf_op jit(solution)/shard_map/all_gather | solution.py:39
  7.9 99.4 %all-gather.6.cloned.1.call-start = ((), (), s32[]{:S(2)}) async-start(), calls=%async_computation | async-start | bytes 1179648 | tf_op jit(solution)/shard_map/all_gather | solution.py:38
  8.7 145.4 %all-gather.12.cloned.1.call-start = ((), (), s32[]{:S(2)}) async-start(), calls=%async_computation.3 | async-start | bytes 1179648 | tf_op jit(solution)/shard_map/all_gather | solution.py:40
  9.4 206.8 %all-gather.10.cloned.1.call-start = ((), (), s32[]{:S(2)}) async-start(), calls=%async_computation.2 | async-start | bytes 1179648 | tf_op jit(solution)/shard_map/all_gather | solution.py:37
  10.0 97.4 %copy-start.5 = (bf16[2,192,1024]{2,1,0:T(8,128)(2,1)S(1)}, bf16[2,192,1024]{2,1,0:T(8,128)(2,1)}, u32[]{:S(2)}) copy-start(bf16[2,192,1024]{2,1,0:T(8,128)(2,1)} %param.13) | copy-start | bytes 2359300
  10.0 939.2 %all-reduce.3.cloned.1.call-start = ((), (), s32[]{:S(2)}) async-start(), calls=%async_computation.4 | async-start | bytes 4194304 | tf_op jit(solution)/shard_map/psum | solution.py:124
  65.1 51.3 %copy-start.11 = (s32[3,9]{1,0:T(4,128)S(1)}, s32[3,9]{1,0:T(4,128)}, u32[]{:S(2)}) copy-start(s32[3,9]{1,0:T(4,128)} %param.20) | copy-start | bytes 328
  110.2 108.6 %collective-permute-start.1 = (bf16[2,192,1024]{2,1,0:T(8,128)(2,1)}, bf16[2,192,1024]{2,1,0:T(8,128)(2,1)S(1)}, u32[]{:S(2)}, u32[]{:S(2)}) collective-permute-start(bf16[2,192,1024]{2,1,0:T(8,128)(2,1)} %pad_maximum_fusion.1), channel_id=1, source_target_pairs={{8,0},{16,8},{24,16},{32,24},{40,32},{48,40},{56,48},{64,56},{72,6... | collective-permute-start | bytes 2359304 | tf_op jit(solution)/shard_map/ppermute | solution.py:19
  111.5 107.3 %collective-permute-start = (bf16[2,192,1024]{2,1,0:T(8,128)(2,1)}, bf16[2,192,1024]{2,1,0:T(8,128)(2,1)}, u32[]{:S(2)}, u32[]{:S(2)}) collective-permute-start(bf16[2,192,1024]{2,1,0:T(8,128)(2,1)} %pad_maximum_fusion.1), channel_id=1, source_target_pairs={{0,8},{8,16},{16,24},{24,32},{32,40},{40,48},{48,56},{56,64},{64,7... | collective-permute-start | bytes 2359304 | tf_op jit(solution)/shard_map/ppermute | solution.py:18
  261.8 871.1 %all-reduce.5.cloned.1.call-start = ((), (), s32[]{:S(2)}) async-start(), calls=%async_computation.5 | async-start | bytes 4194304 | tf_op jit(solution)/shard_map/psum | solution.py:124
  281.9 7.8 copy-start.2
  310.7 7.8 copy-start.2
  339.4 7.8 copy-start.2
  368.2 7.8 copy-start.2
  391.7 1.7 copy-start.4
  393.7 2.1 copy-start.3
  395.8 553.5 %copy-start.7 = (bf16[4,2,192,128]{3,2,1,0:T(8,128)(2,1)S(1)}, bf16[4,2,192,128]{3,2,1,0:T(8,128)(2,1)}, u32[]{:S(2)}) copy-start(bf16[4,2,192,128]{3,2,1,0:T(8,128)(2,1)} %get-tuple-element.94) | copy-start | bytes 1179652
  396.8 555.8 %collective-permute-start.3 = (bf16[2,192,1024]{2,1,0:T(8,128)(2,1)}, bf16[2,192,1024]{2,1,0:T(8,128)(2,1)}, u32[]{:S(2)}, u32[]{:S(2)}) collective-permute-start(bf16[2,192,1024]{2,1,0:T(8,128)(2,1)} %get-tuple-element.247), channel_id=1, source_target_pairs={{8,0},{16,8},{24,16},{32,24},{40,32},{48,40},{56,48},{64,56},{72,6... | collective-permute-start | bytes 2359304 | tf_op jit(solution)/shard_map/ppermute | solution.py:19
  398.1 554.5 %collective-permute-start.2 = (bf16[2,192,1024]{2,1,0:T(8,128)(2,1)S(1)}, bf16[2,192,1024]{2,1,0:T(8,128)(2,1)}, u32[]{:S(2)}, u32[]{:S(2)}) collective-permute-start(bf16[2,192,1024]{2,1,0:T(8,128)(2,1)S(1)} %get-tuple-element.246), channel_id=1, source_target_pairs={{0,8},{8,16},{16,24},{24,32},{32,40},{40,48},{48,56},{56,64},{64,7... | collective-permute-start | bytes 2359304 | tf_op jit(solution)/shard_map/ppermute | solution.py:18
  949.2 2.8 copy-start.9
  952.6 2.3 copy-start.8
  955.0 1.1 copy-start.6
  955.0 1.5 copy-start.10
  956.4 178.2 %copy-start.1 = (bf16[2,192,1024]{2,1,0:T(8,128)(2,1)S(1)}, bf16[2,192,1024]{2,1,0:T(8,128)(2,1)}, u32[]{:S(2)}) copy-start(bf16[2,192,1024]{2,1,0:T(8,128)(2,1)} %param.21) | copy-start | bytes 2359300
Sparse Core Ops, SparseCore 0:
  10.1 52.8 all-gather.7
  65.2 42.0 all-gather.5
  109.5 44.4 all-gather.11
  156.0 60.1 all-gather.9
  262.0 687.2 all-reduce.2
  952.0 180.8 all-reduce.4
